TPU v7x, 128 devices: a whole 4x4x4 slice. The times are simulated.
128 devices in a mesh: sec: 2 (over z_lo), row: 8 (over x, z_hi), col: 8 (over y, core).
Axes of the slice: x: 4, y: 4, z: 4 (z_hi: 2, z_lo: 2; z = z_hi * 2 + z_lo), core: 2. Of those that a mesh axis runs over, the one named last changes fastest.
Arguments:
- held_inverse: bfloat16 [12288, 12288], P('row', ('sec', 'col')), as said below
- factor_panels: bfloat16 [2, 12288, 1024], P(None, ('sec', 'col'), 'row'), may hold values from -0.125 to 0.125
- block_inverses: bfloat16 [2, 1024, 1024], P(None, 'row'), as said below
- covariance: float32 [12288, 12288], P('row', ('sec', 'col')), may hold values from -0.9 to 0.9
Outputs:
- updated: float32 [12288, 12288], P('row', ('sec', 'col'))
Inputs may be any that keep to these rules, and one draw needn't show every extreme that they name: held_inverse is lower triangular with a positive diagonal. Each block of block_inverses is lower triangular with a positive diagonal.
All inputs are finite; a program needn't handle non-finite values.
Results may differ from a plain program's by a relative error of at most 0.0038.
Values may be sent and summed in bfloat16 or wider, within the bound.
A program may use at most 128 MiB of HBM per device.

v0:
```python
import jax
import jax.numpy as jnp
from jax import lax
from jax.sharding import Mesh
from jax.sharding import PartitionSpec as P

PANELS = 2
ROW = ("row_0", "row_1")


def scatter_axes(x, axes, dim):
    for axis in axes:
        x = lax.psum_scatter(x, axis, scatter_dimension=dim, tiled=True)
    return x


def from_root(x, axis, root):
    mine = lax.axis_index(axis) == root
    return lax.psum(jnp.where(mine, x, jnp.zeros_like(x)), axis)


def body(held_inverse, factor_panels, block_inverses, covariance):
    total = covariance
    tile_cols = held_inverse.shape[1]
    groups = lax.axis_size(("sec", "col"))
    ratio = groups // lax.axis_size(ROW)
    column_index = lax.axis_index(("sec", "col"))
    root_row = column_index // ratio
    offset = column_index % ratio * tile_cols
    for panel in range(PANELS):
        partial_value = jnp.dot(
            factor_panels[panel], block_inverses[panel], preferred_element_type=jnp.float32
        )
        scaled = scatter_axes(partial_value, ROW, 1).astype(jnp.bfloat16)
        terms = jnp.dot(
            held_inverse,
            lax.all_gather(scaled, ROW, axis=1, tiled=True),
            preferred_element_type=jnp.float32,
        )
        summed = lax.psum(terms, ("sec", "col"))
        inverse = (-summed).astype(jnp.bfloat16)
        own_block = lax.dynamic_slice_in_dim(inverse, offset, tile_cols, 0)
        column_block = from_root(own_block, ROW, root_row)
        total = total + lax.dot_general(
            inverse, column_block, (((1,), (1,)), ((), ())), preferred_element_type=jnp.float32
        )
    return total


def solution(mesh):
    split = Mesh(
        mesh.devices.reshape(mesh.shape["sec"], 4, 2, mesh.shape["col"]),
        ("sec", "row_0", "row_1", "col"),
    )
    in_specs = (
        P(ROW, ("sec", "col")),
        P(None, ("sec", "col"), ROW),
        P(None, ROW, None),
        P(ROW, ("sec", "col")),
    )
    out_specs = P(ROW, ("sec", "col"))
    return jax.shard_map(body, mesh=split, in_specs=in_specs, out_specs=out_specs, check_vma=False)
```

profile of v0, /device:TPU:5, one launch (start us, length us, event | category | flops | bytes accessed | tf_op | source)
XLA Modules:
  0.0 585.9 jit_solution(17937898365134801965)
XLA Ops:
  6.5 3.4 fusion.2
  10.0 0.0 reduce-scatter.9.cloned.1.call-start
  10.1 2.2 fusion
  12.3 36.8 %reduce-scatter.5.cloned.1.call-done = f32[768,256]{1,0:T(8,128)} async-done(((f32[768,1024]{1,0:T(8,128)}), f32[768,256]{1,0:T(8,128)}) %reduce-scatter.5.cloned.1.call-update) | async-done | bytes 786448 | tf_op jit(solution)/shard_map/reduce_scatter | solution.py:13
  49.2 40.3 %reduce-scatter.9.cloned.1.call-done = f32[768,256]{1,0:T(8,128)} async-done(((f32[768,1024]{1,0:T(8,128)}), f32[768,256]{1,0:T(8,128)}) %reduce-scatter.9.cloned.1.call-update) | async-done | bytes 786448 | tf_op jit(solution)/shard_map/reduce_scatter | solution.py:13
  89.6 25.2 %reduce-scatter.7.cloned.1.call-done = f32[768,128]{1,0:T(8,128)} async-done(((f32[768,256]{1,0:T(8,128)}), f32[768,128]{1,0:T(8,128)}) %reduce-scatter.7.cloned.1.call-update) | async-done | bytes 393232 | tf_op jit(solution)/shard_map/reduce_scatter | solution.py:13
  114.8 1.7 convert_element_type.12
  116.6 0.0 all-gather.5.cloned.1.call-start
  116.6 21.3 %reduce-scatter.11.cloned.1.call-done = f32[768,128]{1,0:T(8,128)} async-done(((f32[768,256]{1,0:T(8,128)}), f32[768,128]{1,0:T(8,128)}) %reduce-scatter.11.cloned.1.call-update) | async-done | bytes 393232 | tf_op jit(solution)/shard_map/reduce_scatter | solution.py:13
  138.0 1.7 convert_element_type.14
  139.7 0.0 all-reduce.5.cloned.1.call-start
  139.7 49.3 %all-gather.3.cloned.1.call-done = bf16[768,1024]{1,0:T(8,128)(2,1)} async-done(((bf16[768,128]{1,0:T(8,128)(2,1)}), bf16[768,1024]{1,0:T(8,128)(2,1)}) %all-gather.3.cloned.1.call-update) | async-done | bytes 1572880 | tf_op jit(solution)/shard_map/all_gather | solution.py:37
  189.0 6.1 %convolution_bitcast_fusion.1 = f32[1536,1024]{0,1:T(8,128)} fusion(bf16[768,1024]{1,0:T(8,128)(2,1)} %all-gather.3.cloned.1.call-done, bf16[1536,768]{1,0:T(8,128)(2,1)S(1)} %copy-done), kind=kOutput, calls=%fused_computation.4 | convolution fusion | flops 2415919104 | bytes 10223616 | tf_op jit(solution)/shard_map/dot_general | solution.py:35
  195.2 47.0 %all-gather.5.cloned.1.call-done = bf16[768,1024]{1,0:T(8,128)(2,1)} async-done(((bf16[768,128]{1,0:T(8,128)(2,1)}), bf16[768,1024]{1,0:T(8,128)(2,1)}) %all-gather.5.cloned.1.call-update) | async-done | bytes 1572880 | tf_op jit(solution)/shard_map/all_gather | solution.py:37
  242.1 6.0 %convolution_bitcast_fusion = f32[1536,1024]{0,1:T(8,128)} fusion(bf16[768,1024]{1,0:T(8,128)(2,1)} %all-gather.5.cloned.1.call-done, bf16[1536,768]{1,0:T(8,128)(2,1)S(1)} %copy-done), kind=kOutput, calls=%fused_computation.3 | convolution fusion | flops 2415919104 | bytes 10223616 | tf_op jit(solution)/shard_map/dot_general | solution.py:35
  248.1 0.0 all-reduce.7.cloned.1.call-start
  248.2 159.2 %all-reduce.5.cloned.1.call-done = (f32[1536,1024]{0,1:T(8,128)}, f32[1536,1024]{0,1:T(8,128)}) async-done(((f32[1536,1024]{0,1:T(8,128)}, f32[1536,1024]{0,1:T(8,128)}), (f32[1536,1024]{0,1:T(8,128)}, f32[1536,1024]{0,1:T(8,128)})) %all-reduce.5.cloned.1.call-update) | async-done | bytes 12582928 | tf_op jit(solution)/shard_map/psum | solution.py:40
  407.4 6.3 %negate_convert_fusion = (bf16[1536,1024]{0,1:T(8,128)(2,1)S(1)}, bf16[1536,1024]{0,1:T(8,128)(2,1)S(1)}) fusion(f32[1536,1024]{0,1:T(8,128)} %get-tuple-element.6, f32[1536,1024]{0,1:T(8,128)} %get-tuple-element.5), kind=kLoop, calls=%fused_computation | loop fusion | flops 6291456 | bytes 18874368 | tf_op jit(solution)/shard_map/convert_element_type | solution.py:41
  413.7 1.7 dynamic-slice_select_fusion.1
  415.4 0.4 copy-done.2
  415.9 1.5 dynamic-slice_select_fusion
  417.4 151.0 %all-reduce.7.cloned.1.call-done = (bf16[768,1024]{0,1:T(8,128)(2,1)}, bf16[768,1024]{0,1:T(8,128)(2,1)}) async-done(((bf16[768,1024]{0,1:T(8,128)(2,1)}, bf16[768,1024]{0,1:T(8,128)(2,1)}), (bf16[768,1024]{0,1:T(8,128)(2,1)}, bf16[768,1024]{0,1:T(8,128)(2,1)})) %all-reduce.7.cloned.1.call-update) | async-done | bytes 3145744 | tf_op jit(solution)/shard_map/psum | solution.py:19
  568.4 4.3 fusion.10
  572.7 6.4 %add_add_fusion = f32[1536,768]{1,0:T(8,128)} fusion(f32[1536,768]{1,0:T(8,128)} %param.7, f32[1536,768]{1,0:T(8,128)S(1)} %fusion.10, bf16[1536,1024]{0,1:T(8,128)(2,1)S(1)} %copy-done.3, bf16[768,1024]{0,1:T(8,128)(2,1)S(1)} %copy-done.6), kind=kOutput, calls=%fused_computation.2 | convolution fusion | flops 2418278400 | bytes 18874368 | tf_op jit(solution)/shard_map/dot_general | solution.py:44
  (25 shorter events, 0.3 us)
Async XLA Ops:
  6.5 182.5 %copy-start = (bf16[1536,768]{1,0:T(8,128)(2,1)S(1)}, bf16[1536,768]{1,0:T(8,128)(2,1)}, u32[]{:S(2)}) copy-start(bf16[1536,768]{1,0:T(8,128)(2,1)} %param.4) | copy-start | bytes 7077892
  6.5 3.5 copy-start.4
  6.5 3.5 copy-start.5
  6.5 42.6 %reduce-scatter.5.cloned.1.call-start = ((), (), s32[]{:S(2)}) async-start(), calls=%async_computation.4 | async-start | bytes 3932160 | tf_op jit(solution)/shard_map/reduce_scatter | solution.py:13
  10.0 79.6 %reduce-scatter.9.cloned.1.call-start = ((), (), s32[]{:S(2)}) async-start(), calls=%async_computation.7 | async-start | bytes 3932160 | tf_op jit(solution)/shard_map/reduce_scatter | solution.py:13
  12.3 102.6 %reduce-scatter.7.cloned.1.call-start = ((), (), s32[]{:S(2)}) async-start(), calls=%async_computation.5 | async-start | bytes 1179648 | tf_op jit(solution)/shard_map/reduce_scatter | solution.py:13
  49.2 88.8 %reduce-scatter.11.cloned.1.call-start = ((), (), s32[]{:S(2)}) async-start(), calls=%async_computation.8 | async-start | bytes 1179648 | tf_op jit(solution)/shard_map/reduce_scatter | solution.py:13
  89.6 99.4 %all-gather.3.cloned.1.call-start = ((), (), s32[]{:S(2)}) async-start(), calls=%async_computation.6 | async-start | bytes 1769472 | tf_op jit(solution)/shard_map/all_gather | solution.py:37
  116.6 125.6 %all-gather.5.cloned.1.call-start = ((), (), s32[]{:S(2)}) async-start(), calls=%async_computation.9 | async-start | bytes 1769472 | tf_op jit(solution)/shard_map/all_gather | solution.py:37
  139.7 267.7 %all-reduce.5.cloned.1.call-start = ((), (), s32[]{:S(2)}) async-start(), calls=%async_computation.10 | async-start | bytes 25165824 | tf_op jit(solution)/shard_map/psum | solution.py:40
  248.1 320.3 %all-reduce.7.cloned.1.call-start = ((), (), s32[]{:S(2)}) async-start(), calls=%async_computation.11 | async-start | bytes 6291456 | tf_op jit(solution)/shard_map/psum | solution.py:19
  413.7 2.2 copy-start.2
  568.4 4.3 copy-start.3
  568.4 4.3 copy-start.6
  572.7 6.4 %copy-start.1 = (bf16[1536,768]{1,0:T(8,128)(2,1)S(1)}, bf16[1536,768]{1,0:T(8,128)(2,1)}, u32[]{:S(2)}) copy-start(bf16[1536,768]{1,0:T(8,128)(2,1)} %param.4) | copy-start | bytes 7077892
Sparse Core Ops, SparseCore 0:
  10.1 38.9 reduce-scatter.4
  51.6 37.9 reduce-scatter.8
  91.9 22.8 reduce-scatter.6
  117.0 20.8 reduce-scatter.10
  140.0 48.9 all-gather.2
  191.0 51.0 all-gather.4
  248.2 159.1 all-reduce.4
  417.5 150.8 all-reduce.6
where the time goes:
time: 586 us
  waiting for transfers between devices  530 us (90%)
  matrix products  28.4 us (5%)
  between operations  13.6 us (2%)
  other arithmetic  12.9 us (2%)
    psum x1, waiting for transfers between devices, body(): summed = lax.psum(terms, ('sec', 'col'))  159 us
    psum x1, waiting for transfers between devices, from_root(): return lax.psum(jnp.where(mine, x, jnp.zeros_like(x)), axis)  151 us
    reduce_scatter x4, waiting for transfers between devices, scatter_axes(): x = lax.psum_scatter(x, axis, scatter_dimension=dim, tiled=True)  124 us
    all_gather x2, waiting for transfers between devices, body(): lax.all_gather(scaled, ROW, axis=1, tiled=True)  96.2 us
    dot_general x2, matrix products, body(): jnp.dot(held_inverse, lax.all_gather(scaled, ROW, axis=1, tiled=True), pr...  12.1 us
  transfers between devices with their start and end apart: 8, of which 8 were waited for; matrix products, arithmetic and copies ran while one was open for 2% of the time, Pallas kernels for 0%

commit v1 on v0

--- a/solution.py
+++ b/solution.py
@@ -37,7 +37,7 @@
             lax.all_gather(scaled, ROW, axis=1, tiled=True),
             preferred_element_type=jnp.float32,
         )
-        summed = lax.psum(terms, ("sec", "col"))
+        summed = lax.psum(lax.psum(terms, "sec"), "col")
         inverse = (-summed).astype(jnp.bfloat16)
         own_block = lax.dynamic_slice_in_dim(inverse, offset, tile_cols, 0)
         column_block = from_root(own_block, ROW, root_row)

time: 586 us -> 869 us (1.48)
  waiting for transfers between devices: 530 us -> 814 us
    psum x1 -> x2, waiting for transfers between devices: 159 us -> 443 us  [body(): summed = lax.psum(lax.psum(terms, 'sec'), 'col')]
  transfers between devices with their start and end apart: 8 -> 9, of which waited for: 8 -> 9; matrix products, arithmetic and copies ran while one was open for 2% -> 1% of each run, Pallas kernels for 0% -> 0%
where the time goes in v1:
time: 869 us
  waiting for transfers between devices  814 us (94%)
  matrix products  28.4 us (3%)
  between operations  13.3 us (2%)
  other arithmetic  12.9 us (1%)
    psum x2, waiting for transfers between devices, body(): summed = lax.psum(lax.psum(terms, 'sec'), 'col')  443 us
    psum x1, waiting for transfers between devices, from_root(): return lax.psum(jnp.where(mine, x, jnp.zeros_like(x)), axis)  150 us
    reduce_scatter x4, waiting for transfers between devices, scatter_axes(): x = lax.psum_scatter(x, axis, scatter_dimension=dim, tiled=True)  124 us
    all_gather x2, waiting for transfers between devices, body(): lax.all_gather(scaled, ROW, axis=1, tiled=True)  96.3 us
  transfers between devices with their start and end apart: 9, of which 9 were waited for; matrix products, arithmetic and copies ran while one was open for 1% of the time, Pallas kernels for 0%

profile of v1, /device:TPU:5, one launch (start us, length us, event | category | flops | bytes accessed | tf_op | source)
XLA Modules:
  0.0 869.0 jit_solution(7928242597934804811)
XLA Ops:
  6.5 3.4 fusion.2
  10.0 0.0 reduce-scatter.9.cloned.1.call-start
  10.1 2.2 fusion
  12.3 36.8 %reduce-scatter.5.cloned.1.call-done = f32[768,256]{1,0:T(8,128)} async-done(((f32[768,1024]{1,0:T(8,128)}), f32[768,256]{1,0:T(8,128)}) %reduce-scatter.5.cloned.1.call-update) | async-done | bytes 786448 | tf_op jit(solution)/shard_map/reduce_scatter | solution.py:13
  49.2 40.3 %reduce-scatter.9.cloned.1.call-done = f32[768,256]{1,0:T(8,128)} async-done(((f32[768,1024]{1,0:T(8,128)}), f32[768,256]{1,0:T(8,128)}) %reduce-scatter.9.cloned.1.call-update) | async-done | bytes 786448 | tf_op jit(solution)/shard_map/reduce_scatter | solution.py:13
  89.6 25.2 %reduce-scatter.7.cloned.1.call-done = f32[768,128]{1,0:T(8,128)} async-done(((f32[768,256]{1,0:T(8,128)}), f32[768,128]{1,0:T(8,128)}) %reduce-scatter.7.cloned.1.call-update) | async-done | bytes 393232 | tf_op jit(solution)/shard_map/reduce_scatter | solution.py:13
  114.8 1.7 convert_element_type.12
  116.6 0.0 all-gather.5.cloned.1.call-start
  116.6 21.3 %reduce-scatter.11.cloned.1.call-done = f32[768,128]{1,0:T(8,128)} async-done(((f32[768,256]{1,0:T(8,128)}), f32[768,128]{1,0:T(8,128)}) %reduce-scatter.11.cloned.1.call-update) | async-done | bytes 393232 | tf_op jit(solution)/shard_map/reduce_scatter | solution.py:13
  138.0 1.7 convert_element_type.14
  139.7 0.0 all-reduce.9.cloned.1.call-start
  139.7 49.3 %all-gather.3.cloned.1.call-done = bf16[768,1024]{1,0:T(8,128)(2,1)} async-done(((bf16[768,128]{1,0:T(8,128)(2,1)}), bf16[768,1024]{1,0:T(8,128)(2,1)}) %all-gather.3.cloned.1.call-update) | async-done | bytes 1572880 | tf_op jit(solution)/shard_map/all_gather | solution.py:37
  189.0 6.0 convolution_bitcast_fusion.1
  195.0 47.1 %all-gather.5.cloned.1.call-done = bf16[768,1024]{1,0:T(8,128)(2,1)} async-done(((bf16[768,128]{1,0:T(8,128)(2,1)}), bf16[768,1024]{1,0:T(8,128)(2,1)}) %all-gather.5.cloned.1.call-update) | async-done | bytes 1572880 | tf_op jit(solution)/shard_map/all_gather | solution.py:37
  242.1 6.1 convolution_bitcast_fusion
  248.3 296.2 %all-reduce.9.cloned.1.call-done = (f32[1536,1024]{0,1:T(8,128)}, f32[1536,1024]{0,1:T(8,128)}) async-done(((f32[1536,1024]{0,1:T(8,128)}, f32[1536,1024]{0,1:T(8,128)}), (f32[1536,1024]{0,1:T(8,128)}, f32[1536,1024]{0,1:T(8,128)})) %all-reduce.9.cloned.1.call-update) | async-done | bytes 12582928 | tf_op jit(solution)/shard_map/psum | solution.py:40
  544.5 146.9 %all-reduce.7.cloned.1.call-done = (f32[1536,1024]{0,1:T(8,128)}, f32[1536,1024]{0,1:T(8,128)}) async-done(((f32[1536,1024]{0,1:T(8,128)}, f32[1536,1024]{0,1:T(8,128)}), (f32[1536,1024]{0,1:T(8,128)}, f32[1536,1024]{0,1:T(8,128)})) %all-reduce.7.cloned.1.call-update) | async-done | bytes 12582928 | tf_op jit(solution)/shard_map/psum | solution.py:40
  691.5 6.3 negate_convert_fusion
  697.8 1.7 dynamic-slice_select_fusion.1
  699.5 0.4 copy-done.2
  700.0 1.5 dynamic-slice_select_fusion
  701.5 150.2 %all-reduce.11.cloned.1.call-done = (bf16[768,1024]{0,1:T(8,128)(2,1)}, bf16[768,1024]{0,1:T(8,128)(2,1)}) async-done(((bf16[768,1024]{0,1:T(8,128)(2,1)}, bf16[768,1024]{0,1:T(8,128)(2,1)}), (bf16[768,1024]{0,1:T(8,128)(2,1)}, bf16[768,1024]{0,1:T(8,128)(2,1)})) %all-reduce.11.cloned.1.call-update) | async-done | bytes 3145744 | tf_op jit(solution)/shard_map/psum | solution.py:19
  851.7 4.3 fusion.10
  856.1 6.3 add_add_fusion
  (28 shorter events, 0.4 us)
Async XLA Ops:
  6.5 182.5 %copy-start = (bf16[1536,768]{1,0:T(8,128)(2,1)S(1)}, bf16[1536,768]{1,0:T(8,128)(2,1)}, u32[]{:S(2)}) copy-start(bf16[1536,768]{1,0:T(8,128)(2,1)} %param.4) | copy-start | bytes 7077892
  6.5 3.5 copy-start.4
  6.5 3.5 copy-start.5
  6.5 42.6 %reduce-scatter.5.cloned.1.call-start = ((), (), s32[]{:S(2)}) async-start(), calls=%async_computation.4 | async-start | bytes 3932160 | tf_op jit(solution)/shard_map/reduce_scatter | solution.py:13
  10.0 79.6 %reduce-scatter.9.cloned.1.call-start = ((), (), s32[]{:S(2)}) async-start(), calls=%async_computation.7 | async-start | bytes 3932160 | tf_op jit(solution)/shard_map/reduce_scatter | solution.py:13
  12.3 102.6 %reduce-scatter.7.cloned.1.call-start = ((), (), s32[]{:S(2)}) async-start(), calls=%async_computation.5 | async-start | bytes 1179648 | tf_op jit(solution)/shard_map/reduce_scatter | solution.py:13
  49.2 88.8 %reduce-scatter.11.cloned.1.call-start = ((), (), s32[]{:S(2)}) async-start(), calls=%async_computation.8 | async-start | bytes 1179648 | tf_op jit(solution)/shard_map/reduce_scatter | solution.py:13
  89.6 99.4 %all-gather.3.cloned.1.call-start = ((), (), s32[]{:S(2)}) async-start(), calls=%async_computation.6 | async-start | bytes 1769472 | tf_op jit(solution)/shard_map/all_gather | solution.py:37
  116.6 125.6 %all-gather.5.cloned.1.call-start = ((), (), s32[]{:S(2)}) async-start(), calls=%async_computation.9 | async-start | bytes 1769472 | tf_op jit(solution)/shard_map/all_gather | solution.py:37
  139.7 404.8 %all-reduce.9.cloned.1.call-start = ((), (), s32[]{:S(2)}) async-start(), calls=%async_computation.11 | async-start | bytes 25165824 | tf_op jit(solution)/shard_map/psum | solution.py:40
  248.2 443.3 %all-reduce.7.cloned.1.call-start = ((), (), s32[]{:S(2)}) async-start(), calls=%async_computation.10 | async-start | bytes 25165824 | tf_op jit(solution)/shard_map/psum | solution.py:40
  544.5 307.2 %all-reduce.11.cloned.1.call-start = ((), (), s32[]{:S(2)}) async-start(), calls=%async_computation.12 | async-start | bytes 6291456 | tf_op jit(solution)/shard_map/psum | solution.py:19
  697.8 2.2 copy-start.2
  851.7 4.3 copy-start.3
  851.7 4.3 copy-start.6
  856.1 6.4 copy-start.1
Sparse Core Ops, SparseCore 0:
  10.1 38.9 reduce-scatter.4
  51.6 37.9 reduce-scatter.8
  91.9 22.8 reduce-scatter.6
  117.0 20.8 reduce-scatter.10
  140.0 48.9 all-gather.2
  191.0 51.0 all-gather.4
  248.3 296.0 all-reduce.8
  546.9 144.5 all-reduce.6
  701.6 150.0 all-reduce.10
